TPU v7x, 256 devices: a whole 4x4x8 slice. The times are simulated.
256 devices in a mesh: dp: 8 (over z_hi, x), space: 32 (over z_lo, y, core).
Axes of the slice: x: 4, y: 4, z: 8 (z_hi: 2, z_lo: 4; z = z_hi * 4 + z_lo), core: 2. Of those that a mesh axis runs over, the one named last changes fastest.
Arguments:
- crop: bfloat16 [8, 4, 128, 64, 64], P('dp', None, 'space'), may hold values from -6 to 6
- filter_one: bfloat16 [3, 3, 3, 4, 32], replicated, may hold values from -0.625 to 0.625
- filter_two: bfloat16 [3, 3, 3, 32, 64], replicated, may hold values from -0.21875 to 0.21875
- cotangent: bfloat16 [8, 64, 32, 16, 16], P('dp', None, 'space'), may hold values from -1 to 1
Outputs:
- features: bfloat16 [8, 64, 32, 16, 16], P('dp', None, 'space')
- grad_one: float32 [3, 3, 3, 4, 32], replicated
- grad_two: float32 [3, 3, 3, 32, 64], replicated
All inputs are finite; a program needn't handle non-finite values.
Results may differ from a plain program's by a relative error of at most 0.0045.
The roundings to bfloat16 on the way count: a program that leaves them out, or rounds other values in their place, can miss the bound.
Values may be sent and summed in bfloat16 or wider, within the bound.
A program may use at most 128 MiB of HBM per device.

v0:
```python
import jax
import jax.numpy as jnp
from jax import lax
from jax.sharding import PartitionSpec as P


def with_halo(shard, sides, width):
    for axis, dim in sides:
        count, length = (lax.axis_size(axis), shard.shape[dim])
        up = [(i, (i + 1) % count) for i in range(count - 1)]
        down = [(j, i) for i, j in up]
        last = lax.slice_in_dim(shard, length - width, length, axis=dim)
        leading = lax.slice_in_dim(shard, 0, width, axis=dim)
        before = lax.ppermute(last, axis, up)
        after = lax.ppermute(leading, axis, down)
        shard = jnp.concatenate([before, shard, after], axis=dim)
    return shard


def leaky(value):
    return jnp.where(value > 0, value, 0.3 * value)


def slope(value):
    return jnp.where(value > 0, 1.0, 0.3)


def pooled(value):
    shape = value.shape
    blocks = value.reshape(shape[0], shape[1], shape[2] // 2, 2, shape[3] // 2, 2, shape[4] // 2, 2)
    return blocks.mean(axis=(3, 5, 7))


def widened(value):
    shape = value.shape
    spread = jnp.broadcast_to(
        value[:, :, :, None, :, None, :, None],
        (shape[0], shape[1], shape[2], 2, shape[3], 2, shape[4], 2),
    )
    return spread.reshape(shape[0], shape[1], 2 * shape[2], 2 * shape[3], 2 * shape[4])


def convolve(source, kernel):
    return lax.conv_general_dilated(
        source,
        kernel,
        (1, 1, 1),
        ((0, 0), (1, 1), (1, 1)),
        dimension_numbers=("NCDHW", "DHWIO", "NCDHW"),
        preferred_element_type=jnp.float32,
    )


def flipped(kernel):
    return jnp.transpose(kernel[::-1, ::-1, ::-1], (0, 1, 2, 4, 3))


def filter_grad(source, gradient):
    planes, extent_y, extent_z = (gradient.shape[2], gradient.shape[3], gradient.shape[4])
    padded = jnp.pad(source, ((0, 0), (0, 0), (0, 0), (1, 1), (1, 1)))
    partials = []
    for offset in range(27):
        shift_a, shift_b, shift_c = (offset // 9, offset // 3 % 3, offset % 3)
        window = padded[
            :,
            :,
            shift_a : shift_a + planes,
            shift_b : shift_b + extent_y,
            shift_c : shift_c + extent_z,
        ]
        partials.append(
            jnp.einsum("bcxyz,bdxyz->cd", window, gradient, preferred_element_type=jnp.float32)
        )
    return jnp.stack(partials).reshape(3, 3, 3, source.shape[1], gradient.shape[1])


def local(crop, filter_one, filter_two, cotangent):
    crop_wide = with_halo(crop, (("space", 2),), 1)
    z_one = convolve(crop_wide, filter_one)
    maps_one = pooled(leaky(z_one)).astype(jnp.bfloat16)
    maps_wide = with_halo(maps_one, (("space", 2),), 1)
    z_two = convolve(maps_wide, filter_two)
    grad_pre_two = (slope(z_two) * widened(cotangent.astype(jnp.float32)) * 0.125).astype(
        jnp.bfloat16
    )
    grad_outer = with_halo(grad_pre_two, (("space", 2),), 1)
    features = pooled(leaky(z_two)).astype(jnp.bfloat16)
    local_two = filter_grad(maps_wide, grad_pre_two)
    back_one = convolve(grad_outer, flipped(filter_two))
    grad_pre_one = (slope(z_one) * widened(back_one) * 0.125).astype(jnp.bfloat16)
    local_one = filter_grad(crop_wide, grad_pre_one)
    grad_one, grad_two = lax.psum((local_one, local_two), ("dp", "space"))
    return (features, grad_one, grad_two)


def solution(mesh):
    placed = (P("dp", None, "space", None, None), P(), P(), P("dp", None, "space", None, None))
    return jax.shard_map(
        local,
        mesh=mesh,
        in_specs=placed,
        out_specs=(P("dp", None, "space", None, None), P(), P()),
        check_vma=False,
    )
```

profile of v0, /device:TPU:1, one launch (start us, length us, event | category | flops | bytes accessed | tf_op | source)
XLA Modules:
  0.0 399.3 jit_solution(16076839817375526808)
XLA Ops:
  8.5 4.6 %collective-permute-start = (bf16[1,4,1,64,64]{4,1,3,2,0:T(4,128)(2,1)S(1)}, bf16[1,4,1,64,64]{4,1,3,2,0:T(4,128)(2,1)S(1)}, u32[]{:S(2)}, u32[]{:S(2)}) collective-permute-start(bf16[1,4,1,64,64]{4,1,3,2,0:T(4,128)(2,1)S(1)} %get-tuple-element.20), channel_id=1, source_target_pairs={{0,1},{1,2},{2,3},{3,4},{4,5},{5,6},{6,7},{7,8},{8,9},{9,10},{10,1... | collective-permute-start | bytes 98312 | tf_op jit(solution)/shard_map/ppermute | solution.py:14
  19.8 3.7 copy.327
  25.2 24.3 %compare_select_fusion = (f32[4,64,8,9,32]{4,2,3,1,0:T(8,128)}, f32[4,64,8,9,32]{4,2,3,1,0:T(8,128)}) fusion(pred[8,9]{0,1:T(8,128)(4,1)S(1)} %copy-done.15, bf16[3,3,3,4,32]{4,3,2,1,0:T(4,128)(2,1)S(1)} %copy-done.14, bf16[4,6,64,1,7,2]{4,0,5,2,1,3:T(4,128)(2,1)S(1)} %slice.254, bf16[4,6,64,1,8,9]{4,0,5,2,1,3:T(4,128)(2,1)} %copy.327), kind=kOutput, calls=%fused_computation.1 | convolution fusion | flops 129835008 | bytes 4989768 | tf_op jit(solution)/shard_map/conv_general_dilated | solution.py:44
  49.5 8.7 %copy.328 = f32[4,64,8,9,32]{1,4,3,2,0:T(8,128)} copy(f32[4,64,8,9,32]{4,2,3,1,0:T(8,128)} %get-tuple-element.10) | data formatting | bytes 4718592 | tf_op jit(solution)/shard_map/jit(_where)/select_n | solution.py:21
  58.2 4.6 %slice_bitcast_fusion.1 = f32[1,32,4,64,64]{3,1,4,2,0:T(8,128)} fusion(f32[4,64,1,72,32]{1,4,3,0,2:T(8,128)} %bitcast.701), kind=kLoop, calls=%fused_computation.14 | loop fusion | bytes 4194304 | tf_op jit(solution)/shard_map/jit(_where)/select_n | solution.py:21
  62.8 9.3 %copy.329 = f32[1,32,4,64,64]{1,4,3,2,0:T(8,128)} copy(f32[1,32,4,64,64]{3,1,4,2,0:T(8,128)} %slice_bitcast_fusion.1) | data formatting | bytes 4194304 | tf_op jit(solution)/shard_map/jit(_where)/select_n | solution.py:21
  72.1 9.1 %reduce_sum.21 = f32[32,2,32,32]{0,3,2,1:T(8,128)S(1)} reduce(f32[32,2,2,32,2,32,2]{0,6,5,4,3,2,1:T(2,128)} %bitcast.698, f32[]{:T(128)} %constant.5.clone.1), dimensions={2,4,6}, to_apply=%region_0.1 | reduce | flops 458752 | bytes 2359300 | tf_op jit(solution)/shard_map/reduce_sum | solution.py:31
  84.4 2.4 collective-permute-start.3
  88.4 8.7 %copy.335 = f32[4,64,8,9,32]{1,4,3,2,0:T(8,128)} copy(f32[4,64,8,9,32]{4,2,3,1,0:T(8,128)} %get-tuple-element.9) | data formatting | bytes 4718592 | tf_op jit(solution)/shard_map/jit(_where)/select_n | solution.py:25
  97.8 2.3 pad_maximum_fusion
  100.1 3.8 copy.455
  103.9 2.6 pad.12.clone
  106.5 3.0 copy.333
  110.7 4.6 %compare_select_fusion.1 = (f32[2,32,8,5,64]{4,2,3,1,0:T(8,128)S(1)}, f32[2,32,8,5,64]{4,2,3,1,0:T(8,128)}) fusion(bf16[3,3,3,32,64]{4,3,2,1,0:T(8,128)(2,1)S(1)} %copy-done, bf16[32,4,32,1,7,2]{0,4,5,2,1,3:T(8,128)(2,1)S(1)} %slice.258, bf16[32,4,32,1,8,5]{0,4,5,2,1,3:T(8,128)(2,1)} %copy.333, pred[8,5]{0,1:T(8,128)(4,1)S(1)} %copy-done.16), kind=kOutput, calls=%fused_computation.34 | convolution fusion | flops 279412736 | bytes 1863720 | tf_op jit(solution)/shard_map/conv_general_dilated | solution.py:44
  136.9 3.1 collective-permute-start.4
  140.0 2.1 collective-permute-start.5
  144.9 2.8 collective-permute-done.5
  148.9 5.1 %fusion.32 = f32[2,32,8,5,32]{4,2,3,1,0:T(8,128)S(1)} fusion(bf16[3,3,3,32,64]{4,3,2,1,0:T(8,128)(2,1)S(1)} %copy-done, bf16[64,4,32,1,7,2]{0,4,5,2,1,3:T(8,128)(2,1)S(1)} %slice.264, bf16[64,4,32,1,8,5]{0,4,5,2,1,3:T(8,128)(2,1)S(1)} %copy.339, pred[8,5]{0,1:T(8,128)(4,1)S(1)} %copy-done.16), kind=kOutput, calls=%fused_computation.36 | convolution fusion | flops 280051712 | bytes 1323048 | tf_op jit(solution)/shard_map/conv_general_dilated | solution.py:44
  155.0 7.6 %broadcast_in_dim.44 = f32[32,2,2,32,2,32,2]{0,6,5,4,3,2,1:T(2,128)} broadcast(f32[32,2,32,32]{0,3,2,1:T(8,128)S(1)} %copy.341), dimensions={0,1,3,5} | broadcast | bytes 2359296 | tf_op jit(solution)/shard_map/broadcast_in_dim | solution.py:36
  162.6 7.8 %copy.342 = f32[1,32,4,64,64]{3,1,4,2,0:T(8,128)} copy(f32[1,32,4,64,64]{1,4,3,2,0:T(8,128)} %bitcast.699) | data formatting | bytes 4194304 | tf_op jit(solution)/shard_map/broadcast_in_dim | solution.py:36
  170.4 5.8 %fusion.14 = bf16[32,4,64,64]{2,0,3,1:T(8,128)(2,1)} fusion(f32[1,32,4,64,64]{3,1,4,2,0:T(8,128)} %copy.342, f32[4,64,1,72,32]{1,4,3,0,2:T(8,128)} %bitcast.700), kind=kLoop, calls=%fused_computation.20 | loop fusion | flops 1572864 | bytes 5242880 | tf_op jit(solution)/shard_map/reshape.3
  176.3 5.7 %copy.343 = bf16[32,4,64,64]{3,0,2,1:T(8,128)(2,1)S(1)} copy(bf16[32,4,64,64]{2,0,3,1:T(8,128)(2,1)} %fusion.14) | data formatting | bytes 2097152 | tf_op jit(solution)/shard_map/reshape.3
  201.1 85.7 %psum.14 = f32[3,3,3,4,32]{4,3,2,1,0:T(4,128)} all-reduce(f32[3,3,3,4,32]{4,3,2,1,0:T(4,128)S(1)} %bitcast.714), channel_id=1, replica_groups=mesh['dp'=8,'space'=32] {'dp','space'}, use_global_device_ids=true, to_apply=%region_3.4 | all-reduce | flops 3456 | bytes 27648 | tf_op jit(solution)/shard_map/psum | solution.py:92
  286.8 103.6 %all-reduce.4.cloned.1.call-done = f32[3,3,3,32,64]{4,3,2,1,0:T(8,128)} async-done(((f32[3,3,3,32,64]{4,3,2,1,0:T(8,128)}), f32[3,3,3,32,64]{4,3,2,1,0:T(8,128)}) %all-reduce.4.cloned.1.call-update) | async-done | bytes 221200 | tf_op jit(solution)/shard_map/psum | solution.py:92
  (130 shorter events, 63.3 us)
Async XLA Ops:
  7.2 103.6 %copy-start = (bf16[3,3,3,32,64]{4,3,2,1,0:T(8,128)(2,1)S(1)}, bf16[3,3,3,32,64]{4,3,2,1,0:T(8,128)(2,1)}, u32[]{:S(2)}) copy-start(bf16[3,3,3,32,64]{4,3,2,1,0:T(8,128)(2,1)} %param.6) | copy-start | bytes 331780
  7.2 383.2 %all-reduce.4.cloned.1.call-start = ((), (), s32[]{:S(2)}) async-start(), calls=%async_computation | async-start | bytes 884736 | tf_op jit(solution)/shard_map/psum | solution.py:92
  8.5 6.5 %collective-permute-start = (bf16[1,4,1,64,64]{4,1,3,2,0:T(4,128)(2,1)S(1)}, bf16[1,4,1,64,64]{4,1,3,2,0:T(4,128)(2,1)S(1)}, u32[]{:S(2)}, u32[]{:S(2)}) collective-permute-start(bf16[1,4,1,64,64]{4,1,3,2,0:T(4,128)(2,1)S(1)} %get-tuple-element.20), channel_id=1, source_target_pairs={{0,1},{1,2},{2,3},{3,4},{4,5},{5,6},{6,7},{7,8},{8,9},{9,10},{10,1... | collective-permute-start | bytes 98312 | tf_op jit(solution)/shard_map/ppermute | solution.py:14
  13.1 5.6 %collective-permute-start.1 = (bf16[1,4,1,64,64]{4,1,3,2,0:T(4,128)(2,1)S(1)}, bf16[1,4,1,64,64]{4,1,3,2,0:T(4,128)(2,1)S(1)}, u32[]{:S(2)}, u32[]{:S(2)}) collective-permute-start(bf16[1,4,1,64,64]{4,1,3,2,0:T(4,128)(2,1)S(1)} %get-tuple-element.19), channel_id=1, source_target_pairs={{1,0},{2,1},{3,2},{4,3},{5,4},{6,5},{7,6},{8,7},{9,8},{10,9},{11,1... | collective-permute-start | bytes 98312 | tf_op jit(solution)/shard_map/ppermute | solution.py:15
  15.0 0.6 copy-start.10
  18.7 0.6 copy-start.8
  19.8 5.4 %copy-start.14 = (bf16[3,3,3,4,32]{4,3,2,1,0:T(4,128)(2,1)S(1)}, bf16[3,3,3,4,32]{4,3,2,1,0:T(4,128)(2,1)}, u32[]{:S(2)}) copy-start(bf16[3,3,3,4,32]{4,3,2,1,0:T(4,128)(2,1)} %param.5) | copy-start | bytes 20740
  19.8 5.4 %copy-start.15 = (pred[8,9]{0,1:T(8,128)(4,1)S(1)}, pred[8,9]{0,1:T(8,128)(4,1)}, u32[]{:S(2)}) copy-start(pred[8,9]{0,1:T(8,128)(4,1)} %constant.39) | copy-start | bytes 220
  81.6 5.2 %copy-start.13 = (bf16[1,64,1,16,16]{1,4,3,2,0:T(8,128)(2,1)S(1)}, bf16[1,64,1,16,16]{1,4,3,2,0:T(8,128)(2,1)}, u32[]{:S(2)}) copy-start(bf16[1,64,1,16,16]{1,4,3,2,0:T(8,128)(2,1)} %param.7) | copy-start | bytes 98308
  81.6 5.9 %copy-start.3 = (bf16[1,4,4,64,64]{4,3,2,1,0:T(8,128)(2,1)S(1)}, bf16[1,4,4,64,64]{4,3,2,1,0:T(8,128)(2,1)}, u32[]{:S(2)}) copy-start(bf16[1,4,4,64,64]{4,3,2,1,0:T(8,128)(2,1)} %param.4) | copy-start | bytes 393220
  82.5 14.6 %collective-permute-start.2 = (bf16[1,32,1,32,32]{4,1,3,2,0:T(8,128)(2,1)}, bf16[1,32,1,32,32]{4,1,3,2,0:T(8,128)(2,1)S(1)}, u32[]{:S(2)}, u32[]{:S(2)}) collective-permute-start(bf16[1,32,1,32,32]{4,1,3,2,0:T(8,128)(2,1)} %get-tuple-element.17), channel_id=1, source_target_pairs={{0,1},{1,2},{2,3},{3,4},{4,5},{5,6},{6,7},{7,8},{8,9},{9,10},{10,1... | collective-permute-start | bytes 196616 | tf_op jit(solution)/shard_map/ppermute | solution.py:14
  84.4 13.4 %collective-permute-start.3 = (bf16[1,32,1,32,32]{4,1,3,2,0:T(8,128)(2,1)S(1)}, bf16[1,32,1,32,32]{4,1,3,2,0:T(8,128)(2,1)}, u32[]{:S(2)}, u32[]{:S(2)}) collective-permute-start(bf16[1,32,1,32,32]{4,1,3,2,0:T(8,128)(2,1)S(1)} %get-tuple-element.18), channel_id=1, source_target_pairs={{1,0},{2,1},{3,2},{4,3},{5,4},{6,5},{7,6},{8,7},{9,8},{10,9},{11,1... | collective-permute-start | bytes 196616 | tf_op jit(solution)/shard_map/ppermute | solution.py:15
  97.1 0.7 copy-start.6
  106.5 4.2 %copy-start.16 = (pred[8,5]{0,1:T(8,128)(4,1)S(1)}, pred[8,5]{0,1:T(8,128)(4,1)}, u32[]{:S(2)}) copy-start(pred[8,5]{0,1:T(8,128)(4,1)} %constant.38) | copy-start | bytes 124
  115.4 0.9 copy-start.4
  118.3 1.9 copy-start.7
  134.8 2.0 copy-start.2
  136.0 0.8 copy-start.5
  136.9 8.1 %collective-permute-start.4 = (bf16[1,64,1,32,32]{1,3,4,2,0:T(8,128)(2,1)S(1)}, bf16[1,64,1,32,32]{1,3,4,2,0:T(8,128)(2,1)S(1)}, u32[]{:S(2)}, u32[]{:S(2)}) collective-permute-start(bf16[1,64,1,32,32]{1,3,4,2,0:T(8,128)(2,1)S(1)} %get-tuple-element.15), channel_id=1, source_target_pairs={{0,1},{1,2},{2,3},{3,4},{4,5},{5,6},{6,7},{7,8},{8,9},{9,10},{10,1... | collective-permute-start | bytes 393224 | tf_op jit(solution)/shard_map/ppermute | solution.py:14
  140.0 7.7 %collective-permute-start.5 = (bf16[1,64,1,32,32]{1,3,4,2,0:T(8,128)(2,1)S(1)}, bf16[1,64,1,32,32]{1,3,4,2,0:T(8,128)(2,1)S(1)}, u32[]{:S(2)}, u32[]{:S(2)}) collective-permute-start(bf16[1,64,1,32,32]{1,3,4,2,0:T(8,128)(2,1)S(1)} %get-tuple-element.16), channel_id=1, source_target_pairs={{1,0},{2,1},{3,2},{4,3},{5,4},{6,5},{7,6},{8,7},{9,8},{10,9},{11,1... | collective-permute-start | bytes 393224 | tf_op jit(solution)/shard_map/ppermute | solution.py:15
  183.3 1.5 copy-start.11
  189.6 1.6 copy-start.1
  189.6 1.6 copy-start.12
  196.1 1.5 copy-start.9
Sparse Core Ops, SparseCore 0:
  136.9 253.4 all-reduce.3
where the time goes:
time: 407 us; the launch traced here: 399 us
  waiting for transfers between devices  108 us (27%)
  blocking collectives  85.7 us (21%)
  local copies, waits for them, and re-layouts  83.9 us (21%)
  matrix products  71.1 us (17%)
  other arithmetic  19.3 us (5%)
  starting transfers between devices  16.1 us (4%)
  between operations  14.9 us (4%)
    psum x1, waiting for transfers between devices, local(): grad_one, grad_two = lax.psum((local_one, local_two), ('dp', 'space'))  104 us
    psum x1, blocking collectives, local(): grad_one, grad_two = lax.psum((local_one, local_two), ('dp', 'space'))  85.7 us
    dot_general x54, matrix products, filter_grad(): jnp.einsum('bcxyz,bdxyz->cd', window, gradient, preferred_element_type=jn...  37.1 us
    conv_general_dilated x3, matrix products, convolve(): lax.conv_general_dilated(source, kernel, (1, 1, 1), ((0, 0), (1, 1), (1,...  34 us
    select_n x4, local copies, waits for them, and re-layouts, leaky(): return jnp.where(value > 0, value, 0.3 * value)  24.2 us
    broadcast_in_dim x6, local copies, waits for them, and re-layouts, widened(): jnp.broadcast_to(value[:, :, :, None, :, None, :, None], (shape[0], shape...  17.1 us
    unnamed x41, local copies, waits for them, and re-layouts  12.5 us
    conv_general_dilated x7, local copies, waits for them, and re-layouts, convolve(): lax.conv_general_dilated(source, kernel, (1, 1, 1), ((0, 0), (1, 1), (1,...  10.5 us
  transfers between devices with their start and end apart: 7, of which 3 were waited for; matrix products, arithmetic and copies ran while one was open for 17% of the time, Pallas kernels for 0%

commit v1 on v0

--- a/solution.py
+++ b/solution.py
@@ -2,6 +2,14 @@
 import jax.numpy as jnp
 from jax import lax
 from jax.sharding import PartitionSpec as P
+
+
+def form_local_data(raw):
+    bus_axis = "space"
+    device_axis = "dp"
+    for to_i in (device_axis, bus_axis):
+        raw = lax.psum(raw, to_i)
+    return raw
 
 
 def with_halo(shard, sides, width):
@@ -89,7 +97,7 @@
     back_one = convolve(grad_outer, flipped(filter_two))
     grad_pre_one = (slope(z_one) * widened(back_one) * 0.125).astype(jnp.bfloat16)
     local_one = filter_grad(crop_wide, grad_pre_one)
-    grad_one, grad_two = lax.psum((local_one, local_two), ("dp", "space"))
+    grad_one, grad_two = form_local_data((local_one, local_two))
     return (features, grad_one, grad_two)
 
 

time: 407 us -> 532 us (1.31)
  blocking collectives: 85.7 us -> 181 us
  waiting for transfers between devices: 108 us -> 138 us
    psum x1 -> x2, blocking collectives: 85.7 us -> 181 us  [form_local_data(): raw = lax.psum(raw, to_i)]
    psum x1 -> x2, waiting for transfers between devices: 104 us -> 133 us  [form_local_data(): raw = lax.psum(raw, to_i)]
  transfers between devices with their start and end apart: 7 -> 8, of which waited for: 3 -> 4; matrix products, arithmetic and copies ran while one was open for 17% -> 13% of each run, Pallas kernels for 0% -> 0%
where the time goes in v1:
time: 532 us; the launch traced here: 524 us
  blocking collectives  181 us (34%)
  waiting for transfers between devices  138 us (26%)
  local copies, waits for them, and re-layouts  83.9 us (16%)
  matrix products  71.1 us (13%)
  other arithmetic  19.3 us (4%)
  starting transfers between devices  16.2 us (3%)
  between operations  14.9 us (3%)
    psum x2, blocking collectives, form_local_data(): raw = lax.psum(raw, to_i)  181 us
    psum x2, waiting for transfers between devices, form_local_data(): raw = lax.psum(raw, to_i)  133 us
    dot_general x54, matrix products, filter_grad(): jnp.einsum('bcxyz,bdxyz->cd', window, gradient, preferred_element_type=jn...  37.1 us
    conv_general_dilated x3, matrix products, convolve(): lax.conv_general_dilated(source, kernel, (1, 1, 1), ((0, 0), (1, 1), (1,...  34 us
    select_n x4, local copies, waits for them, and re-layouts, leaky(): return jnp.where(value > 0, value, 0.3 * value)  24.2 us
    broadcast_in_dim x6, local copies, waits for them, and re-layouts, widened(): jnp.broadcast_to(value[:, :, :, None, :, None, :, None], (shape[0], shape...  17.1 us
    unnamed x41, local copies, waits for them, and re-layouts  12.5 us
  transfers between devices with their start and end apart: 8, of which 4 were waited for; matrix products, arithmetic and copies ran while one was open for 13% of the time, Pallas kernels for 0%

profile of v1, /device:TPU:1, one launch (start us, length us, event | category | flops | bytes accessed | tf_op | source)
XLA Modules:
  0.0 524.3 jit_solution(18237478992681271443)
XLA Ops:
  8.5 4.6 collective-permute-start
  19.8 3.7 copy.327
  25.2 24.2 %compare_select_fusion = (f32[4,64,8,9,32]{4,2,3,1,0:T(8,128)}, f32[4,64,8,9,32]{4,2,3,1,0:T(8,128)}) fusion(pred[8,9]{0,1:T(8,128)(4,1)S(1)} %copy-done.15, bf16[3,3,3,4,32]{4,3,2,1,0:T(4,128)(2,1)S(1)} %copy-done.14, bf16[4,6,64,1,7,2]{4,0,5,2,1,3:T(4,128)(2,1)S(1)} %slice.254, bf16[4,6,64,1,8,9]{4,0,5,2,1,3:T(4,128)(2,1)} %copy.327), kind=kOutput, calls=%fused_computation.1 | convolution fusion | flops 129835008 | bytes 4989768 | tf_op jit(solution)/shard_map/conv_general_dilated | solution.py:52
  49.5 8.7 %copy.328 = f32[4,64,8,9,32]{1,4,3,2,0:T(8,128)} copy(f32[4,64,8,9,32]{4,2,3,1,0:T(8,128)} %get-tuple-element.10) | data formatting | bytes 4718592 | tf_op jit(solution)/shard_map/jit(_where)/select_n | solution.py:29
  58.1 4.6 slice_bitcast_fusion.1
  62.7 9.3 %copy.329 = f32[1,32,4,64,64]{1,4,3,2,0:T(8,128)} copy(f32[1,32,4,64,64]{3,1,4,2,0:T(8,128)} %slice_bitcast_fusion.1) | data formatting | bytes 4194304 | tf_op jit(solution)/shard_map/jit(_where)/select_n | solution.py:29
  72.1 9.1 %reduce_sum.21 = f32[32,2,32,32]{0,3,2,1:T(8,128)S(1)} reduce(f32[32,2,2,32,2,32,2]{0,6,5,4,3,2,1:T(2,128)} %bitcast.698, f32[]{:T(128)} %constant.5.clone.1), dimensions={2,4,6}, to_apply=%region_0.1 | reduce | flops 458752 | bytes 2359300 | tf_op jit(solution)/shard_map/reduce_sum | solution.py:39
  84.3 2.4 collective-permute-start.3
  88.3 8.7 %copy.335 = f32[4,64,8,9,32]{1,4,3,2,0:T(8,128)} copy(f32[4,64,8,9,32]{4,2,3,1,0:T(8,128)} %get-tuple-element.9) | data formatting | bytes 4718592 | tf_op jit(solution)/shard_map/jit(_where)/select_n | solution.py:33
  100.0 3.8 copy.455
  103.9 2.6 pad.12.clone
  106.4 3.0 copy.333
  110.6 4.6 compare_select_fusion.1
  136.8 3.1 collective-permute-start.4
  144.9 2.8 collective-permute-done.5
  148.8 5.1 fusion.32
  154.9 7.6 %broadcast_in_dim.44 = f32[32,2,2,32,2,32,2]{0,6,5,4,3,2,1:T(2,128)} broadcast(f32[32,2,32,32]{0,3,2,1:T(8,128)S(1)} %copy.341), dimensions={0,1,3,5} | broadcast | bytes 2359296 | tf_op jit(solution)/shard_map/broadcast_in_dim | solution.py:44
  162.5 7.8 %copy.342 = f32[1,32,4,64,64]{3,1,4,2,0:T(8,128)} copy(f32[1,32,4,64,64]{1,4,3,2,0:T(8,128)} %bitcast.699) | data formatting | bytes 4194304 | tf_op jit(solution)/shard_map/broadcast_in_dim | solution.py:44
  170.3 5.8 %fusion.14 = bf16[32,4,64,64]{2,0,3,1:T(8,128)(2,1)} fusion(f32[1,32,4,64,64]{3,1,4,2,0:T(8,128)} %copy.342, f32[4,64,1,72,32]{1,4,3,0,2:T(8,128)} %bitcast.700), kind=kLoop, calls=%fused_computation.20 | loop fusion | flops 1572864 | bytes 5242880 | tf_op jit(solution)/shard_map/reshape.3
  176.2 5.7 %copy.343 = bf16[32,4,64,64]{3,0,2,1:T(8,128)(2,1)S(1)} copy(bf16[32,4,64,64]{2,0,3,1:T(8,128)(2,1)} %fusion.14) | data formatting | bytes 2097152 | tf_op jit(solution)/shard_map/reshape.3
  200.3 43.0 %all-reduce.5.cloned.1.call-done = f32[3,3,3,32,64]{4,3,2,1,0:T(8,128)} async-done(((f32[3,3,3,32,64]{4,3,2,1,0:T(8,128)}), f32[3,3,3,32,64]{4,3,2,1,0:T(8,128)}) %all-reduce.5.cloned.1.call-update) | async-done | bytes 221200 | tf_op jit(solution)/shard_map/psum | solution.py:11
  244.1 41.8 %psum.28 = f32[3,3,3,4,32]{4,3,2,1,0:T(4,128)S(1)} all-reduce(f32[3,3,3,4,32]{4,3,2,1,0:T(4,128)S(1)} %bitcast.714), channel_id=1, replica_groups=mesh['dp'=8,'space'=32] {'dp'}, use_global_device_ids=true, to_apply=%region_3.4 | all-reduce | flops 3456 | bytes 27648 | tf_op jit(solution)/shard_map/psum | solution.py:11
  285.9 139.4 %psum.29 = f32[3,3,3,4,32]{4,3,2,1,0:T(4,128)} all-reduce(f32[3,3,3,4,32]{4,3,2,1,0:T(4,128)S(1)} %psum.28), channel_id=1, replica_groups=mesh['dp'=8,'space'=32] {'space'}, use_global_device_ids=true, to_apply=%region_4.5 | all-reduce | flops 3456 | bytes 27648 | tf_op jit(solution)/shard_map/psum | solution.py:11
  425.3 90.1 %all-reduce.7.cloned.1.call-done = f32[3,3,3,32,64]{4,3,2,1,0:T(8,128)} async-done(((f32[3,3,3,32,64]{4,3,2,1,0:T(8,128)}), f32[3,3,3,32,64]{4,3,2,1,0:T(8,128)}) %all-reduce.7.cloned.1.call-update) | async-done | bytes 221200 | tf_op jit(solution)/shard_map/psum | solution.py:11
  (134 shorter events, 67.7 us)
Async XLA Ops:
  7.2 103.5 %copy-start = (bf16[3,3,3,32,64]{4,3,2,1,0:T(8,128)(2,1)S(1)}, bf16[3,3,3,32,64]{4,3,2,1,0:T(8,128)(2,1)}, u32[]{:S(2)}) copy-start(bf16[3,3,3,32,64]{4,3,2,1,0:T(8,128)(2,1)} %param.6) | copy-start | bytes 331780
  7.2 236.2 %all-reduce.5.cloned.1.call-start = ((), (), s32[]{:S(2)}) async-start(), calls=%async_computation | async-start | bytes 884736 | tf_op jit(solution)/shard_map/psum | solution.py:11
  8.5 6.5 %collective-permute-start = (bf16[1,4,1,64,64]{4,1,3,2,0:T(4,128)(2,1)S(1)}, bf16[1,4,1,64,64]{4,1,3,2,0:T(4,128)(2,1)S(1)}, u32[]{:S(2)}, u32[]{:S(2)}) collective-permute-start(bf16[1,4,1,64,64]{4,1,3,2,0:T(4,128)(2,1)S(1)} %get-tuple-element.20), channel_id=1, source_target_pairs={{0,1},{1,2},{2,3},{3,4},{4,5},{5,6},{6,7},{7,8},{8,9},{9,10},{10,1... | collective-permute-start | bytes 98312 | tf_op jit(solution)/shard_map/ppermute | solution.py:22
  13.1 5.6 %collective-permute-start.1 = (bf16[1,4,1,64,64]{4,1,3,2,0:T(4,128)(2,1)S(1)}, bf16[1,4,1,64,64]{4,1,3,2,0:T(4,128)(2,1)S(1)}, u32[]{:S(2)}, u32[]{:S(2)}) collective-permute-start(bf16[1,4,1,64,64]{4,1,3,2,0:T(4,128)(2,1)S(1)} %get-tuple-element.19), channel_id=1, source_target_pairs={{1,0},{2,1},{3,2},{4,3},{5,4},{6,5},{7,6},{8,7},{9,8},{10,9},{11,1... | collective-permute-start | bytes 98312 | tf_op jit(solution)/shard_map/ppermute | solution.py:23
  15.0 0.6 copy-start.10
  19.8 5.4 %copy-start.14 = (bf16[3,3,3,4,32]{4,3,2,1,0:T(4,128)(2,1)S(1)}, bf16[3,3,3,4,32]{4,3,2,1,0:T(4,128)(2,1)}, u32[]{:S(2)}) copy-start(bf16[3,3,3,4,32]{4,3,2,1,0:T(4,128)(2,1)} %param.5) | copy-start | bytes 20740
  19.8 5.4 %copy-start.15 = (pred[8,9]{0,1:T(8,128)(4,1)S(1)}, pred[8,9]{0,1:T(8,128)(4,1)}, u32[]{:S(2)}) copy-start(pred[8,9]{0,1:T(8,128)(4,1)} %constant.39) | copy-start | bytes 220
  81.5 5.2 copy-start.13
  81.5 5.9 %copy-start.3 = (bf16[1,4,4,64,64]{4,3,2,1,0:T(8,128)(2,1)S(1)}, bf16[1,4,4,64,64]{4,3,2,1,0:T(8,128)(2,1)}, u32[]{:S(2)}) copy-start(bf16[1,4,4,64,64]{4,3,2,1,0:T(8,128)(2,1)} %param.4) | copy-start | bytes 393220
  82.4 14.6 %collective-permute-start.2 = (bf16[1,32,1,32,32]{4,1,3,2,0:T(8,128)(2,1)}, bf16[1,32,1,32,32]{4,1,3,2,0:T(8,128)(2,1)S(1)}, u32[]{:S(2)}, u32[]{:S(2)}) collective-permute-start(bf16[1,32,1,32,32]{4,1,3,2,0:T(8,128)(2,1)} %get-tuple-element.17), channel_id=1, source_target_pairs={{0,1},{1,2},{2,3},{3,4},{4,5},{5,6},{6,7},{7,8},{8,9},{9,10},{10,1... | collective-permute-start | bytes 196616 | tf_op jit(solution)/shard_map/ppermute | solution.py:22
  84.3 13.4 %collective-permute-start.3 = (bf16[1,32,1,32,32]{4,1,3,2,0:T(8,128)(2,1)S(1)}, bf16[1,32,1,32,32]{4,1,3,2,0:T(8,128)(2,1)}, u32[]{:S(2)}, u32[]{:S(2)}) collective-permute-start(bf16[1,32,1,32,32]{4,1,3,2,0:T(8,128)(2,1)S(1)} %get-tuple-element.18), channel_id=1, source_target_pairs={{1,0},{2,1},{3,2},{4,3},{5,4},{6,5},{7,6},{8,7},{9,8},{10,9},{11,1... | collective-permute-start | bytes 196616 | tf_op jit(solution)/shard_map/ppermute | solution.py:23
  97.0 0.7 copy-start.6
  106.4 4.2 copy-start.16
  115.3 0.9 copy-start.4
  118.2 1.9 copy-start.7
  134.6 2.1 copy-start.2
  135.9 0.8 copy-start.5
  136.7 378.7 %all-reduce.7.cloned.1.call-start = ((), (), s32[]{:S(2)}) async-start(), calls=%async_computation.1 | async-start | bytes 884736 | tf_op jit(solution)/shard_map/psum | solution.py:11
  136.8 8.1 %collective-permute-start.4 = (bf16[1,64,1,32,32]{1,3,4,2,0:T(8,128)(2,1)S(1)}, bf16[1,64,1,32,32]{1,3,4,2,0:T(8,128)(2,1)S(1)}, u32[]{:S(2)}, u32[]{:S(2)}) collective-permute-start(bf16[1,64,1,32,32]{1,3,4,2,0:T(8,128)(2,1)S(1)} %get-tuple-element.15), channel_id=1, source_target_pairs={{0,1},{1,2},{2,3},{3,4},{4,5},{5,6},{6,7},{7,8},{8,9},{9,10},{10,1... | collective-permute-start | bytes 393224 | tf_op jit(solution)/shard_map/ppermute | solution.py:22
  139.9 7.7 %collective-permute-start.5 = (bf16[1,64,1,32,32]{1,3,4,2,0:T(8,128)(2,1)S(1)}, bf16[1,64,1,32,32]{1,3,4,2,0:T(8,128)(2,1)S(1)}, u32[]{:S(2)}, u32[]{:S(2)}) collective-permute-start(bf16[1,64,1,32,32]{1,3,4,2,0:T(8,128)(2,1)S(1)} %get-tuple-element.16), channel_id=1, source_target_pairs={{1,0},{2,1},{3,2},{4,3},{5,4},{6,5},{7,6},{8,7},{9,8},{10,9},{11,1... | collective-permute-start | bytes 393224 | tf_op jit(solution)/shard_map/ppermute | solution.py:23
  183.2 1.5 copy-start.11
  189.6 1.6 copy-start.1
  189.6 1.6 copy-start.12
  196.1 1.5 copy-start.9
  (1 other events, 0.6 us)
Sparse Core Ops, SparseCore 0:
  136.8 106.5 all-reduce.4
  246.2 269.1 all-reduce.6
